TPU v7x, 32 devices: a whole 2x2x4 slice. The times are simulated.
32 devices in a mesh: fsdp: 4 (over x, core), seq: 8 (over z, y).
Axes of the slice: x: 2, y: 2, z: 4, core: 2. Of those that a mesh axis runs over, the one named last changes fastest.
Arguments:
- tokens: bfloat16 [4, 56, 28, 512], P('fsdp', 'seq'), may hold values from -6 to 6
- cotangent: bfloat16 [4, 56, 28, 512], P('fsdp', 'seq'), may hold values from -6 to 6
- region_ids: int32 [56, 28], replicated, may hold values from 0 to 3
- relative_index: int32 [49, 49], replicated, may hold values from 0 to 168, as said below
- first_gain: bfloat16 [512], P('fsdp'), may hold values from 0.5 to 1.5
- first_offset: bfloat16 [512], P('fsdp'), may hold values from -3 to 3
- qkv_weight: bfloat16 [512, 1536], P('fsdp'), may hold values from -0.25 to 0.25
- proj_weight: bfloat16 [512, 512], P('fsdp'), may hold values from -0.75 to 0.75
- bias_table: bfloat16 [16, 169], P('fsdp'), may hold values from -4 to 4
- second_gain: bfloat16 [512], P('fsdp'), may hold values from 0.5 to 1.5
- second_offset: bfloat16 [512], P('fsdp'), may hold values from -3 to 3
- expand_weight: bfloat16 [512, 2048], P('fsdp'), may hold values from -0.25 to 0.25
- reduce_weight: bfloat16 [2048, 512], P('fsdp'), may hold values from -0.125 to 0.125
Outputs:
- output: bfloat16 [4, 56, 28, 512], P('fsdp', 'seq')
- tokens_grad: float32 [4, 56, 28, 512], P('fsdp', 'seq')
- first_gain_grad: float32 [512], P('fsdp')
- first_offset_grad: float32 [512], P('fsdp')
- qkv_weight_grad: float32 [512, 1536], P('fsdp')
- proj_weight_grad: float32 [512, 512], P('fsdp')
- bias_table_grad: float32 [16, 169], P('fsdp')
- second_gain_grad: float32 [512], P('fsdp')
- second_offset_grad: float32 [512], P('fsdp')
- expand_weight_grad: float32 [512, 2048], P('fsdp')
- reduce_weight_grad: float32 [2048, 512], P('fsdp')
Inputs may be any that keep to these rules, and one draw needn't show every extreme that they name: relative_index[i, j] depends only on the row and column offsets between positions i and j of a 7 x 7 window, and distinct offsets give distinct entries.
All inputs are finite; a program needn't handle non-finite values.
Results may differ from a plain program's by a relative error of at most 0.018.
Values may be sent and summed in bfloat16 or wider, within the bound.
A program may use at most 128 MiB of HBM per device.

v0:
```python
import jax
import jax.numpy as jnp
from jax import lax
from jax.sharding import PartitionSpec as P

WS = 7
SHIFT = 3
EPSILON = 1e-05
MASKED = -100.0
SQRT_HALF = 0.7071067811865476
INV_ROOT_TAU = 0.3989422804014327


def layer_norm(values, norm_gain, norm_offset):
    average = jnp.mean(values, axis=-1, keepdims=True)
    centred = values - average
    variance = jnp.mean(centred * centred, axis=-1, keepdims=True)
    inverse = lax.rsqrt(variance + EPSILON)
    normed = centred * inverse
    return (normed * norm_gain + norm_offset, normed, inverse)


def norm_back(upstream, normed, inverse, norm_gain):
    scaled = upstream * norm_gain
    mean_grad = jnp.mean(scaled, axis=-1, keepdims=True)
    second = jnp.mean(scaled * normed, axis=-1, keepdims=True)
    grad_in = inverse * (scaled - mean_grad - normed * second)
    lead_axes = tuple(range(upstream.ndim - 1))
    return (grad_in, jnp.sum(upstream * normed, axis=lead_axes), jnp.sum(upstream, axis=lead_axes))


def gelu_parts(hidden):
    normal_cdf = 0.5 * (1.0 + jax.scipy.special.erf(hidden * SQRT_HALF))
    density = jnp.exp(-0.5 * hidden * hidden) * INV_ROOT_TAU
    return (hidden * normal_cdf, normal_cdf + hidden * density)


def to_windows(field_in, num_heads):
    lead_dims = field_in.shape[:-3]
    num_rows, num_cols, features = field_in.shape[-3:]
    lead_count = len(lead_dims)
    pieces = field_in.reshape(
        lead_dims + (num_rows // WS, WS, num_cols // WS, WS, num_heads, features // num_heads)
    )
    axis_order = tuple(range(lead_count)) + (
        lead_count,
        lead_count + 2,
        lead_count + 4,
        lead_count + 1,
        lead_count + 3,
        lead_count + 5,
    )
    return pieces.transpose(axis_order).reshape(
        lead_dims + (num_rows // WS, num_cols // WS, num_heads, WS * WS, features // num_heads)
    )


def from_windows(window_tiles):
    lead_dims = window_tiles.shape[:-5]
    win_rows, win_cols, num_heads, positions, head_dim = window_tiles.shape[-5:]
    lead_count = len(lead_dims)
    pieces = window_tiles.reshape(lead_dims + (win_rows, win_cols, num_heads, WS, WS, head_dim))
    axis_order = tuple(range(lead_count)) + (
        lead_count,
        lead_count + 3,
        lead_count + 1,
        lead_count + 4,
        lead_count + 2,
        lead_count + 5,
    )
    return pieces.transpose(axis_order).reshape(
        lead_dims + (win_rows * WS, win_cols * WS, num_heads * head_dim)
    )


def make_mask(regions):
    num_rows, num_cols = regions.shape
    region_tiles = (
        regions.reshape(num_rows // WS, WS, num_cols // WS, WS)
        .transpose(0, 2, 1, 3)
        .reshape(num_rows // WS, num_cols // WS, WS * WS)
    )
    same_region = region_tiles[..., :, None] == region_tiles[..., None, :]
    return jnp.where(same_region, 0.0, MASKED).astype(jnp.float32)


def one_hot_index(relative_index, entries):
    return (relative_index[..., None] == jnp.arange(entries, dtype=jnp.int32)).astype(jnp.float32)


def table_bias(table_rows, relative_index):
    onehot = one_hot_index(relative_index, table_rows.shape[-1])
    return jnp.einsum("ijr,hr->hij", onehot, table_rows, precision=lax.Precision.HIGHEST)


def table_grad(bias_grad, relative_index, entries):
    onehot = one_hot_index(relative_index, entries)
    return jnp.einsum("hij,ijr->hr", bias_grad, onehot, precision=lax.Precision.HIGHEST)


def attend_forward(qkv_field, rel_bias, mask_add, num_heads):
    rolled = jnp.roll(qkv_field, -SHIFT, axis=-2)
    window_tiles = to_windows(rolled, num_heads)
    queries, key_tiles, value_tiles = (window_tiles[:, 0], window_tiles[:, 1], window_tiles[:, 2])
    scores = (
        jnp.einsum("bxyhid,bxyhjd->bxyhij", queries, key_tiles, preferred_element_type=jnp.float32)
        + rel_bias
        + mask_add[:, :, None]
    )
    exp_scores = jnp.exp(scores)
    row_total = jnp.sum(exp_scores, axis=-1, keepdims=True)
    attn_probs = (exp_scores / row_total).astype(jnp.bfloat16)
    attn_tiles = jnp.einsum(
        "bxyhij,bxyhjd->bxyhid", attn_probs, value_tiles, preferred_element_type=jnp.float32
    ).astype(jnp.bfloat16)
    field_out = jnp.roll(from_windows(attn_tiles), SHIFT, axis=-2)
    return (field_out, (queries, key_tiles, value_tiles, jnp.log(row_total)))


def attend_backward(grad_field, kept_state, rel_bias, mask_add, num_heads):
    queries, key_tiles, value_tiles, log_total = kept_state
    grad_tiles = to_windows(jnp.roll(grad_field, -SHIFT, axis=-2), num_heads)
    scores = (
        jnp.einsum("bxyhid,bxyhjd->bxyhij", queries, key_tiles, preferred_element_type=jnp.float32)
        + rel_bias
        + mask_add[:, :, None]
    )
    probs_back = jnp.exp(scores - log_total)
    value_grad = jnp.einsum(
        "bxyhij,bxyhid->bxyhjd",
        probs_back.astype(jnp.bfloat16),
        grad_tiles,
        preferred_element_type=jnp.float32,
    )
    prob_grad = jnp.einsum(
        "bxyhid,bxyhjd->bxyhij", grad_tiles, value_tiles, preferred_element_type=jnp.float32
    )
    score_grad = probs_back * (prob_grad - jnp.sum(probs_back * prob_grad, axis=-1, keepdims=True))
    score_low = score_grad.astype(jnp.bfloat16)
    query_scale = queries.shape[-1] ** (-0.5)
    query_grad = (
        jnp.einsum(
            "bxyhij,bxyhjd->bxyhid", score_low, key_tiles, preferred_element_type=jnp.float32
        )
        * query_scale
    )
    key_grad = jnp.einsum(
        "bxyhij,bxyhid->bxyhjd", score_low, queries, preferred_element_type=jnp.float32
    )
    stacked = jnp.stack([query_grad, key_grad, value_grad], axis=1).astype(jnp.bfloat16)
    field_grad = jnp.roll(from_windows(stacked), SHIFT, axis=-2)
    return (field_grad, jnp.sum(score_grad, axis=(0, 1, 2)))


def shards(
    tokens,
    cotangent,
    region_ids,
    relative_index,
    first_gain,
    first_offset,
    qkv_weight,
    proj_weight,
    bias_table,
    second_gain,
    second_offset,
    expand_weight,
    reduce_weight,
):
    gathered = (
        lax.all_gather(first_gain, "fsdp", axis=0, tiled=True),
        lax.all_gather(first_offset, "fsdp", axis=0, tiled=True),
        lax.all_gather(qkv_weight, "fsdp", axis=0, tiled=True),
        lax.all_gather(proj_weight, "fsdp", axis=0, tiled=True),
        lax.all_gather(bias_table, "fsdp", axis=0, tiled=True),
        lax.all_gather(second_gain, "fsdp", axis=0, tiled=True),
        lax.all_gather(second_offset, "fsdp", axis=0, tiled=True),
        lax.all_gather(expand_weight, "fsdp", axis=0, tiled=True),
        lax.all_gather(reduce_weight, "fsdp", axis=0, tiled=True),
    )
    gain_one = gathered[0].astype(jnp.float32)
    offset_one = gathered[1].astype(jnp.float32)
    qkv_full = gathered[2]
    proj_full = gathered[3]
    table_full = gathered[4].astype(jnp.float32)
    gain_two = gathered[5].astype(jnp.float32)
    offset_two = gathered[6].astype(jnp.float32)
    expand_full = gathered[7]
    reduce_full = gathered[8]
    num_images, num_rows, num_cols, width = tokens.shape
    num_heads, entries = table_full.shape
    query_scale = (width // num_heads) ** (-0.5)
    factors = jnp.array([query_scale, 1.0, 1.0], dtype=jnp.float32).reshape(1, 3, 1, 1, 1)
    qkv_cols = qkv_full.reshape(width, 3, width)
    inputs = tokens.astype(jnp.float32)
    normed_one, hat_one, inv_one = layer_norm(inputs, gain_one, offset_one)
    first_low = normed_one.astype(jnp.bfloat16)
    per_device = num_heads // lax.axis_size("seq")
    head_start = lax.axis_index("seq") * per_device
    qkv_local = (
        jnp.einsum("brwc,ctd->btrwd", first_low, qkv_cols, preferred_element_type=jnp.float32)
        * factors
    ).astype(jnp.bfloat16)
    qkv_heads = lax.all_to_all(qkv_local, "seq", split_axis=4, concat_axis=2, tiled=True)
    qkv_heads = jnp.roll(qkv_heads, -SHIFT, axis=2)
    rel_bias = table_bias(
        lax.dynamic_slice_in_dim(table_full, head_start, per_device, 0), relative_index
    )
    mask_add = make_mask(region_ids)
    attn_heads, kept_state = attend_forward(qkv_heads, rel_bias, mask_add, per_device)
    attn_heads = jnp.roll(attn_heads, SHIFT, axis=1)
    attended = lax.all_to_all(attn_heads, "seq", split_axis=1, concat_axis=3, tiled=True)
    middle = inputs + jnp.einsum(
        "brwc,cd->brwd", attended, proj_full, preferred_element_type=jnp.float32
    )
    normed_two, hat_two, inv_two = layer_norm(middle, gain_two, offset_two)
    second_low = normed_two.astype(jnp.bfloat16)
    hidden = jnp.einsum(
        "brwc,cf->brwf", second_low, expand_full, preferred_element_type=jnp.float32
    )
    activated, slope = gelu_parts(hidden)
    act_low = activated.astype(jnp.bfloat16)
    output = (
        middle
        + jnp.einsum("brwf,fc->brwc", act_low, reduce_full, preferred_element_type=jnp.float32)
    ).astype(jnp.bfloat16)
    reduce_grad = jnp.einsum(
        "brwf,brwc->fc", act_low, cotangent, preferred_element_type=jnp.float32
    )
    hidden_grad = (
        jnp.einsum("brwc,fc->brwf", cotangent, reduce_full, preferred_element_type=jnp.float32)
        * slope
    ).astype(jnp.bfloat16)
    expand_grad = jnp.einsum(
        "brwc,brwf->cf", second_low, hidden_grad, preferred_element_type=jnp.float32
    )
    upstream_two = jnp.einsum(
        "brwf,cf->brwc", hidden_grad, expand_full, preferred_element_type=jnp.float32
    )
    back_two, gain_two_grad, offset_two_grad = norm_back(upstream_two, hat_two, inv_two, gain_two)
    middle_grad = cotangent.astype(jnp.float32) + back_two
    middle_low = middle_grad.astype(jnp.bfloat16)
    proj_grad = jnp.einsum(
        "brwc,brwd->cd", attended, middle_low, preferred_element_type=jnp.float32
    )
    attended_grad = jnp.einsum(
        "brwd,cd->brwc", middle_low, proj_full, preferred_element_type=jnp.float32
    ).astype(jnp.bfloat16)
    grad_heads = lax.all_to_all(attended_grad, "seq", split_axis=3, concat_axis=1, tiled=True)
    grad_heads = jnp.roll(grad_heads, -SHIFT, axis=1)
    qkv_grad_heads, bias_grad = attend_backward(
        grad_heads, kept_state, rel_bias, mask_add, per_device
    )
    qkv_grad_heads = jnp.roll(qkv_grad_heads, SHIFT, axis=2)
    qkv_grad = lax.all_to_all(qkv_grad_heads, "seq", split_axis=2, concat_axis=4, tiled=True)
    table_part = table_grad(bias_grad, relative_index, entries)
    table_grads = lax.dynamic_update_slice(
        jnp.zeros((num_heads, entries), jnp.float32), table_part, (head_start, 0)
    )
    qkv_grad_w = jnp.einsum(
        "brwc,btrwd->ctd", first_low, qkv_grad, preferred_element_type=jnp.float32
    ).reshape(width, 3 * width)
    upstream_one = jnp.einsum(
        "btrwd,ctd->brwc", qkv_grad, qkv_cols, preferred_element_type=jnp.float32
    )
    back_one, gain_one_grad, offset_one_grad = norm_back(upstream_one, hat_one, inv_one, gain_one)
    tokens_grad = middle_grad + back_one
    shares = (
        lax.psum_scatter(
            gain_one_grad.astype(jnp.bfloat16), "fsdp", scatter_dimension=0, tiled=True
        ).astype(jnp.float32),
        lax.psum_scatter(
            offset_one_grad.astype(jnp.bfloat16), "fsdp", scatter_dimension=0, tiled=True
        ).astype(jnp.float32),
        lax.psum_scatter(
            qkv_grad_w.astype(jnp.bfloat16), "fsdp", scatter_dimension=0, tiled=True
        ).astype(jnp.float32),
        lax.psum_scatter(
            proj_grad.astype(jnp.bfloat16), "fsdp", scatter_dimension=0, tiled=True
        ).astype(jnp.float32),
        lax.psum_scatter(
            table_grads.astype(jnp.bfloat16), "fsdp", scatter_dimension=0, tiled=True
        ).astype(jnp.float32),
        lax.psum_scatter(
            gain_two_grad.astype(jnp.bfloat16), "fsdp", scatter_dimension=0, tiled=True
        ).astype(jnp.float32),
        lax.psum_scatter(
            offset_two_grad.astype(jnp.bfloat16), "fsdp", scatter_dimension=0, tiled=True
        ).astype(jnp.float32),
        lax.psum_scatter(
            expand_grad.astype(jnp.bfloat16), "fsdp", scatter_dimension=0, tiled=True
        ).astype(jnp.float32),
        lax.psum_scatter(
            reduce_grad.astype(jnp.bfloat16), "fsdp", scatter_dimension=0, tiled=True
        ).astype(jnp.float32),
    )
    totals = (
        lax.psum(shares[0].astype(jnp.bfloat16), "seq").astype(jnp.float32),
        lax.psum(shares[1].astype(jnp.bfloat16), "seq").astype(jnp.float32),
        lax.psum(shares[2].astype(jnp.bfloat16), "seq").astype(jnp.float32),
        lax.psum(shares[3].astype(jnp.bfloat16), "seq").astype(jnp.float32),
        lax.psum(shares[4].astype(jnp.bfloat16), "seq").astype(jnp.float32),
        lax.psum(shares[5].astype(jnp.bfloat16), "seq").astype(jnp.float32),
        lax.psum(shares[6].astype(jnp.bfloat16), "seq").astype(jnp.float32),
        lax.psum(shares[7].astype(jnp.bfloat16), "seq").astype(jnp.float32),
        lax.psum(shares[8].astype(jnp.bfloat16), "seq").astype(jnp.float32),
    )
    qkv_total = totals[2]
    proj_total = totals[3]
    expand_total = totals[7]
    reduce_total = totals[8]
    return (
        output,
        tokens_grad,
        totals[0],
        totals[1],
        qkv_total,
        proj_total,
        totals[4],
        totals[5],
        totals[6],
        expand_total,
        reduce_total,
    )


def solution(mesh):
    placed = (
        P("fsdp", "seq", None, None),
        P("fsdp", "seq", None, None),
        P(),
        P(),
        P("fsdp"),
        P("fsdp"),
        P("fsdp", None),
        P("fsdp", None),
        P("fsdp", None),
        P("fsdp"),
        P("fsdp"),
        P("fsdp", None),
        P("fsdp", None),
    )
    return jax.shard_map(
        shards,
        mesh=mesh,
        in_specs=placed,
        out_specs=(
            P("fsdp", "seq", None, None),
            P("fsdp", "seq", None, None),
            P("fsdp"),
            P("fsdp"),
            P("fsdp", None),
            P("fsdp", None),
            P("fsdp", None),
            P("fsdp"),
            P("fsdp"),
            P("fsdp", None),
            P("fsdp", None),
        ),
        check_vma=False,
    )
```

profile of v0, /device:TPU:0, one launch (start us, length us, event | category | flops | bytes accessed | tf_op | source)
XLA Modules:
  0.0 359.1 jit_solution(13753991665746310214)
XLA Ops:
  7.2 2.0 copy.98
  10.0 6.2 %all-gather = bf16[4,1,128]{2,1,0:T(2,128)(2,1)S(1)} all-gather(bf16[1,1,128]{2,1,0:T(2,128)(2,1)} %bitcast.275), channel_id=1, replica_groups=mesh['fsdp'=4,'seq'=8] {'fsdp'}, dimensions={0}, use_global_device_ids=true | all-gather | bytes 1280 | tf_op jit(solution)/shard_map/all_gather | solution.py:171
  16.2 5.4 %all-gather.1 = bf16[4,1,128]{2,1,0:T(2,128)(2,1)S(1)} all-gather(bf16[1,1,128]{2,1,0:T(2,128)(2,1)} %bitcast.276), channel_id=1, replica_groups=mesh['fsdp'=4,'seq'=8] {'fsdp'}, dimensions={0}, use_global_device_ids=true | all-gather | bytes 1280 | tf_op jit(solution)/shard_map/all_gather | solution.py:172
  22.0 10.7 %all-gather.9.cloned.1.call-done = bf16[512,1536]{0,1:T(8,128)(2,1)} async-done(((bf16[128,1536]{0,1:T(8,128)(2,1)}), bf16[512,1536]{0,1:T(8,128)(2,1)}) %all-gather.9.cloned.1.call-update) | async-done | bytes 1572880 | tf_op jit(solution)/shard_map/all_gather | solution.py:173
  32.7 2.9 fusion.22
  35.6 3.7 %copy.100 = bf16[1,3,7,28,512]{3,2,1,0,4:T(8,128)(2,1)S(1)} copy(bf16[1,3,7,28,512]{4,3,1,2,0:T(8,128)(2,1)} %fusion.22) | data formatting | bytes 1204224 | tf_op jit(solution)/shard_map/convert_element_type | solution.py:203
  39.4 4.6 %reshape.406 = bf16[8,2,18816]{2,1,0:T(2,128)(2,1)} reshape(bf16[512,1,3,7,28]{4,3,2,1,0:T(8,128)(2,1)S(1)} %bitcast.239) | data formatting | bytes 1204224
  44.0 5.6 %all-to-all-start = ((bf16[8,2,18816]{2,1,0:T(2,128)(2,1)}), bf16[8,2,18816]{2,1,0:T(2,128)(2,1)}, u32[]{:S(2)}, u32[]{:S(2)}) async-start(bf16[8,2,18816]{2,1,0:T(2,128)(2,1)} %reshape.406), calls=%async_computation | async-start | bytes 1204224 | tf_op jit(solution)/shard_map/all_to_all | solution.py:204
  50.4 5.4 %all-gather.2 = bf16[4,4,169]{2,1,0:T(4,128)(2,1)S(1)} all-gather(bf16[1,4,169]{2,1,0:T(4,128)(2,1)S(1)} %bitcast.272), channel_id=1, replica_groups=mesh['fsdp'=4,'seq'=8] {'fsdp'}, dimensions={0}, use_global_device_ids=true | all-gather | bytes 6760 | tf_op jit(solution)/shard_map/all_gather | solution.py:175
  57.2 1.2 compare_select_fusion
  58.4 7.9 %all-to-all-done = bf16[8,2,18816]{2,1,0:T(2,128)(2,1)} async-done(((bf16[8,2,18816]{2,1,0:T(2,128)(2,1)}), bf16[8,2,18816]{2,1,0:T(2,128)(2,1)}, u32[]{:S(2)}, u32[]{:S(2)}) %all-to-all-start) | async-done | bytes 602144 | tf_op jit(solution)/shard_map/all_to_all | solution.py:204
  66.3 5.0 %reshape.407 = bf16[512,1,3,7,28]{4,3,2,1,0:T(8,128)(2,1)S(1)} reshape(bf16[8,2,18816]{2,1,0:T(2,128)(2,1)} %all-to-all-done) | data formatting | bytes 1204224
  71.3 4.5 %copy.101 = bf16[1,3,7,28,8,64]{5,2,4,3,1,0:T(8,128)(2,1)} copy(bf16[1,3,7,28,8,64]{3,2,1,5,4,0:T(8,128)(2,1)S(1)} %bitcast.238) | data formatting | bytes 1204224 | tf_op jit(solution)/shard_map/all_to_all | solution.py:204
  75.8 2.4 all_to_all.51
  79.1 1.3 fusion.27
  80.4 4.3 %reshape.357 = bf16[1,3,8,7,4,7,2,32]{7,6,3,2,5,4,1,0:T(2,128)(2,1)S(1)} reshape(bf16[1,3,56,28,64]{4,2,3,1,0:T(8,128)(2,1)} %fusion.27) | data formatting | bytes 1204224 | tf_op jit(solution)/shard_map/reshape | solution.py:42
  85.1 1.5 copy.151
  88.1 2.2 exponential_reduce_fusion
  90.9 1.2 convolution_convert_fusion.2
  92.1 1.6 copy.111
  93.7 1.5 copy.112
  95.2 2.2 reshape.364
  98.7 3.7 %all-to-all-start.1 = ((bf16[8,2,6272]{2,1,0:T(2,128)(2,1)}), bf16[8,2,6272]{2,1,0:T(2,128)(2,1)S(1)}, u32[]{:S(2)}, u32[]{:S(2)}) async-start(bf16[8,2,6272]{2,1,0:T(2,128)(2,1)} %reshape.408), calls=%async_computation.1 | async-start | bytes 401408 | tf_op jit(solution)/shard_map/all_to_all | solution.py:212
  102.4 5.1 %all-gather.3 = bf16[4,1,128]{2,1,0:T(2,128)(2,1)S(1)} all-gather(bf16[1,1,128]{2,1,0:T(2,128)(2,1)S(1)} %bitcast.277), channel_id=1, replica_groups=mesh['fsdp'=4,'seq'=8] {'fsdp'}, dimensions={0}, use_global_device_ids=true | all-gather | bytes 1280 | tf_op jit(solution)/shard_map/all_gather | solution.py:176
  107.4 5.0 %all-gather.4 = bf16[4,1,128]{2,1,0:T(2,128)(2,1)S(1)} all-gather(bf16[1,1,128]{2,1,0:T(2,128)(2,1)S(1)} %bitcast.278), channel_id=1, replica_groups=mesh['fsdp'=4,'seq'=8] {'fsdp'}, dimensions={0}, use_global_device_ids=true | all-gather | bytes 1280 | tf_op jit(solution)/shard_map/all_gather | solution.py:177
  112.5 7.9 %all_gather.31 = bf16[512,512]{1,0:T(8,128)(2,1)S(1)} all-gather(bf16[128,512]{1,0:T(8,128)(2,1)S(1)} %copy-done.22), channel_id=1, replica_groups=mesh['fsdp'=4,'seq'=8] {'fsdp'}, dimensions={0}, use_global_device_ids=true | all-gather | bytes 655360 | tf_op jit(solution)/shard_map/all_gather | solution.py:174
  121.9 4.0 %multiply_convert_fusion = (bf16[7,28,2048]{2,1,0:T(8,128)(2,1)}, f32[7,28,2048]{2,1,0:T(8,128)}) fusion(bf16[512,2048]{1,0:T(8,128)(2,1)} %all-gather.11.cloned.1.call-done, f32[1,7,28,512]{3,2,1,0:T(8,128)S(1)} %get-tuple-element.85, f32[512]{0:T(512)S(1)} %bitcast.270, f32[512]{0:T(512)S(1)} %bitcast.260, f32[7,28]{1,0:T(8,128)S(1)} %add_rsqrt_fusion, ...), kind=kOutput, calls=%fused_computation.25 | convolution fusion | flops 413550592 | bytes 4912672 | tf_op jit(solution)/shard_map/brwc,cf->brwf/dot_general | solution.py:218
  125.9 3.3 fusion.3
  129.3 1.4 fusion.64
  131.5 1.1 fusion.21
  132.7 3.4 bitcast_convert_fusion.1
  137.0 3.3 bitcast_convert_fusion
  140.3 1.0 fusion.35
  141.4 1.7 copy.116
  143.1 1.9 reshape.410
  145.0 5.9 %all-to-all-start.2 = ((bf16[8,2,6272]{2,1,0:T(2,128)(2,1)}), bf16[8,2,6272]{2,1,0:T(2,128)(2,1)S(1)}, u32[]{:S(2)}, u32[]{:S(2)}) async-start(bf16[8,2,6272]{2,1,0:T(2,128)(2,1)} %reshape.410), calls=%async_computation.2 | async-start | bytes 401408 | tf_op jit(solution)/shard_map/all_to_all | solution.py:249
  151.2 1.4 log.8
  152.6 6.9 %all-to-all-done.2 = bf16[8,2,6272]{2,1,0:T(2,128)(2,1)S(1)} async-done(((bf16[8,2,6272]{2,1,0:T(2,128)(2,1)}), bf16[8,2,6272]{2,1,0:T(2,128)(2,1)S(1)}, u32[]{:S(2)}, u32[]{:S(2)}) %all-to-all-start.2) | async-done | bytes 200736 | tf_op jit(solution)/shard_map/all_to_all | solution.py:249
  159.5 1.1 reshape.411
  160.6 1.9 copy.117
  162.5 1.2 all_to_all.58
  165.4 1.8 copy.119
  167.2 1.4 convolution_convert_fusion
  168.6 2.4 copy.126
  173.3 1.5 copy.121
  174.8 1.4 convolution_convert_fusion.1
  176.2 1.7 copy.123
  178.5 1.9 copy.127
  180.3 2.3 reshape.371
  185.5 19.8 %all_to_all.66 = bf16[8,2,18816]{2,1,0:T(2,128)(2,1)S(1)} all-to-all(bf16[8,2,18816]{2,1,0:T(2,128)(2,1)S(1)} %reshape.412), channel_id=1, replica_groups=mesh['fsdp'=4,'seq'=8] {'seq'}, dimensions={0} | all-to-all | bytes 1204224 | tf_op jit(solution)/shard_map/all_to_all | solution.py:255
  209.1 2.0 fusion
  213.1 9.0 %reduce-scatter.11.cloned.1.call-done = bf16[512,512]{1,0:T(8,128)(2,1)} async-done(((bf16[2048,512]{1,0:T(8,128)(2,1)}), bf16[512,512]{1,0:T(8,128)(2,1)}) %reduce-scatter.11.cloned.1.call-update) | async-done | bytes 524304 | tf_op jit(solution)/shard_map/reduce_scatter | solution.py:293
  222.1 30.6 %reduce-scatter.5.cloned.1.call-done = bf16[128,1536]{1,0:T(8,128)(2,1)} async-done(((bf16[512,1536]{1,0:T(8,128)(2,1)}), bf16[128,1536]{1,0:T(8,128)(2,1)}) %reduce-scatter.5.cloned.1.call-update) | async-done | bytes 393232 | tf_op jit(solution)/shard_map/reduce_scatter | solution.py:275
  252.7 2.9 fusion.32
  255.8 1.1 fusion.37
  256.9 2.1 fusion.62
  259.1 10.5 %all-reduce.7 = (bf16[512]{0:T(512)(128)(2,1)S(1)}, bf16[512]{0:T(512)(128)(2,1)S(1)}, bf16[16,169]{1,0:T(8,128)(2,1)S(1)}, bf16[512]{0:T(512)(128)(2,1)S(1)}, bf16[512]{0:T(512)(128)(2,1)S(1)}) all-reduce(bf16[512]{0:T(512)(128)(2,1)S(1)} %get-tuple-element.57, ...), channel_id=2, replica_groups=mesh['fsdp'=4,'seq'=8] {'fsdp'}, use_global_device_ids=true, to_apply=%region_11.12.clone | all-reduce | flops 4752 | bytes 19008
  270.0 21.9 %all-reduce.5 = (bf16[128]{0:T(256)(128)(2,1)S(1)}, bf16[128]{0:T(256)(128)(2,1)S(1)}, bf16[4,169]{1,0:T(4,128)(2,1)S(1)}, bf16[128]{0:T(256)(128)(2,1)S(1)}, bf16[128]{0:T(256)(128)(2,1)S(1)}) all-reduce(bf16[128]{0:T(256)(128)(2,1)S(1)} %dynamic-slice.1, ...), channel_id=1, replica_groups=mesh['fsdp'=4,'seq'=8] {'seq'}, use_global_device_ids=true, to_apply=%region_12.13 | all-reduce | flops 1188 | bytes 4752 | tf_op jit(solution)/shard_map/psum | solution.py:298
  294.7 1.2 copy.134
  295.9 50.3 %all-reduce.10.cloned.1.call-done = (bf16[128,1536]{1,0:T(8,128)(2,1)}, bf16[128,512]{1,0:T(8,128)(2,1)}, bf16[128,2048]{1,0:T(8,128)(2,1)}, bf16[512,512]{1,0:T(8,128)(2,1)}) async-done(((bf16[128,1536]{1,0:T(8,128)(2,1)}, bf16[128,512]{1,0:T(8,128)(2,1)}, bf16[128,2048]{1,0:T(8,128)(2,1)}, bf16[512,512]{1,0:T(8,128)(2,1)}), (bf16[128,1536]{1,0:T(8,128)(2,1)}, bf16[128,512]{1,0:T(8,128)(2,1)}, ...) | async-done | bytes 1572880 | tf_op jit(solution)/shard_map/psum | solution.py:300
  346.2 1.7 convert_element_type.178
  347.9 2.0 convert_element_type.176
  349.9 1.1 convert_element_type.186
  351.0 1.1 convert_element_type.188
  (170 shorter events, 26.6 us)
Async XLA Ops:
  7.2 25.5 %copy-start.34 = (f32[3]{0:T(128)S(1)}, f32[3]{0:T(128)}, u32[]{:S(2)}) copy-start(f32[3]{0:T(128)} %constant.41.clone) | copy-start | bytes 40
  7.2 14.5 %copy-start.7 = (bf16[1,7,28,512]{3,2,1,0:T(8,128)(2,1)S(1)}, bf16[1,7,28,512]{3,2,1,0:T(8,128)(2,1)}, u32[]{:S(2)}) copy-start(bf16[1,7,28,512]{3,2,1,0:T(8,128)(2,1)} %param.14) | copy-start | bytes 602116
  7.2 25.5 %all-gather.9.cloned.1.call-start = ((), (), s32[]{:S(2)}) async-start(), calls=%async_computation.8 | async-start | bytes 1966080 | tf_op jit(solution)/shard_map/all_gather | solution.py:173
  9.2 112.7 %all-gather.11.cloned.1.call-start = ((), (), s32[]{:S(2)}) async-start(), calls=%async_computation.9 | async-start | bytes 2621440 | tf_op jit(solution)/shard_map/all_gather | solution.py:178
  21.6 11.1 %copy-start.26 = (f32[4,1,128]{2,1,0:T(1,128)}, f32[4,1,128]{2,1,0:T(1,128)S(1)}, u32[]{:S(2)}) copy-start(f32[4,1,128]{2,1,0:T(1,128)S(1)} %convert_element_type.190) | copy-start | bytes 6148
  39.4 11.0 %copy-start.25 = (bf16[4,169]{1,0:T(4,128)(2,1)S(1)}, bf16[4,169]{1,0:T(4,128)(2,1)}, u32[]{:S(2)}) copy-start(bf16[4,169]{1,0:T(4,128)(2,1)} %param.22) | copy-start | bytes 4060
  39.4 16.4 %copy-start.31 = (s32[49,49]{1,0:T(8,128)S(1)}, s32[49,49]{1,0:T(8,128)}, u32[]{:S(2)}) copy-start(s32[49,49]{1,0:T(8,128)} %param.17) | copy-start | bytes 28816
  44.0 12.7 %copy-start.23 = (s32[56,28]{0,1:T(8,128)S(1)}, s32[56,28]{0,1:T(8,128)}, u32[]{:S(2)}) copy-start(s32[56,28]{0,1:T(8,128)} %param.16) | copy-start | bytes 18820
  44.0 22.3 %all-to-all-start = ((bf16[8,2,18816]{2,1,0:T(2,128)(2,1)}), bf16[8,2,18816]{2,1,0:T(2,128)(2,1)}, u32[]{:S(2)}, u32[]{:S(2)}) async-start(bf16[8,2,18816]{2,1,0:T(2,128)(2,1)} %reshape.406), calls=%async_computation | async-start | bytes 1204224 | tf_op jit(solution)/shard_map/all_to_all | solution.py:204
  49.6 76.3 %all-gather.13.cloned.1.call-start = ((), (), s32[]{:S(2)}) async-start(), calls=%async_computation.10 | async-start | bytes 2621440 | tf_op jit(solution)/shard_map/all_gather | solution.py:179
  87.3 2.9 copy-start.2
  88.1 2.2 copy-start
  88.1 2.8 copy-start.13
  90.3 0.6 copy-start.21
  97.4 5.0 %copy-start.29 = (bf16[128]{0:T(256)(128)(2,1)S(1)}, bf16[128]{0:T(256)(128)(2,1)}, u32[]{:S(2)}) copy-start(bf16[128]{0:T(256)(128)(2,1)} %param.23) | copy-start | bytes 772
  97.4 10.1 %copy-start.30 = (bf16[128]{0:T(256)(128)(2,1)S(1)}, bf16[128]{0:T(256)(128)(2,1)}, u32[]{:S(2)}) copy-start(bf16[128]{0:T(256)(128)(2,1)} %param.24) | copy-start | bytes 772
  97.4 15.1 %copy-start.22 = (bf16[128,512]{1,0:T(8,128)(2,1)S(1)}, bf16[128,512]{1,0:T(8,128)(2,1)}, u32[]{:S(2)}) copy-start(bf16[128,512]{1,0:T(8,128)(2,1)} %param.21) | copy-start | bytes 393220
  98.7 21.8 %all-to-all-start.1 = ((bf16[8,2,6272]{2,1,0:T(2,128)(2,1)}), bf16[8,2,6272]{2,1,0:T(2,128)(2,1)S(1)}, u32[]{:S(2)}, u32[]{:S(2)}) async-start(bf16[8,2,6272]{2,1,0:T(2,128)(2,1)} %reshape.408), calls=%async_computation.1 | async-start | bytes 401408 | tf_op jit(solution)/shard_map/all_to_all | solution.py:212
  102.3 110.7 %reduce-scatter.7.cloned.1.call-start = ((), (), s32[]{:S(2)}) async-start(), calls=%async_computation.12 | async-start | bytes 655360 | tf_op jit(solution)/shard_map/reduce_scatter | solution.py:278
  112.5 8.8 %copy-start.8 = (bf16[1,7,28,512]{3,2,1,0:T(8,128)(2,1)S(1)}, bf16[1,7,28,512]{3,2,1,0:T(8,128)(2,1)}, u32[]{:S(2)}) copy-start(bf16[1,7,28,512]{3,2,1,0:T(8,128)(2,1)} %param.14) | copy-start | bytes 602116
  121.9 4.0 %copy-start.18 = (bf16[1,7,28,512]{3,2,1,0:T(8,128)(2,1)S(1)}, bf16[1,7,28,512]{3,2,1,0:T(8,128)(2,1)}, u32[]{:S(2)}) copy-start(bf16[1,7,28,512]{3,2,1,0:T(8,128)(2,1)} %param.15) | copy-start | bytes 602116
  125.9 3.3 copy-start.12
  129.2 1.4 copy-start.35
  129.3 2.0 copy-start.19
  131.5 8.8 %copy-start.4 = (f32[1,7,28,512]{3,2,1,0:T(8,128)}, f32[1,7,28,512]{3,2,1,0:T(8,128)S(1)}, u32[]{:S(2)}) copy-start(f32[1,7,28,512]{3,2,1,0:T(8,128)S(1)} %fusion.67) | copy-start | bytes 1204228
  132.7 80.4 %reduce-scatter.9.cloned.1.call-start = ((), (), s32[]{:S(2)}) async-start(), calls=%async_computation.13 | async-start | bytes 2621440 | tf_op jit(solution)/shard_map/reduce_scatter | solution.py:290
  136.1 0.9 copy-start.20
  136.1 86.0 %reduce-scatter.11.cloned.1.call-start = ((), (), s32[]{:S(2)}) async-start(), calls=%async_computation.14 | async-start | bytes 2621440 | tf_op jit(solution)/shard_map/reduce_scatter | solution.py:293
  145.0 14.5 %all-to-all-start.2 = ((bf16[8,2,6272]{2,1,0:T(2,128)(2,1)}), bf16[8,2,6272]{2,1,0:T(2,128)(2,1)S(1)}, u32[]{:S(2)}, u32[]{:S(2)}) async-start(bf16[8,2,6272]{2,1,0:T(2,128)(2,1)} %reshape.410), calls=%async_computation.2 | async-start | bytes 401408 | tf_op jit(solution)/shard_map/all_to_all | solution.py:249
  150.9 101.7 %reduce-scatter.5.cloned.1.call-start = ((), (), s32[]{:S(2)}) async-start(), calls=%async_computation.11 | async-start | bytes 1966080 | tf_op jit(solution)/shard_map/reduce_scatter | solution.py:275
  164.1 3.1 copy-start.15
  167.2 3.8 %copy-start.14 = (bf16[1,1,8,4,2,49,32]{5,6,4,3,2,1,0:T(8,128)(2,1)S(1)}, bf16[1,1,8,4,2,49,32]{5,6,4,3,2,1,0:T(8,128)(2,1)}, u32[]{:S(2)}) copy-start(bf16[1,1,8,4,2,49,32]{5,6,4,3,2,1,0:T(8,128)(2,1)} %copy.151) | copy-start | bytes 602116
  171.9 1.0 copy-start.3
  172.5 2.3 copy-start.1
  174.8 3.1 copy-start.10
  176.2 1.7 copy-start.11
  182.7 0.9 slice-start
  182.7 1.3 slice-start.1
  207.7 1.4 copy-start.9
  207.7 1.4 copy-start.27
  209.1 2.1 copy-start.33
  211.1 41.6 %copy-start.6 = (bf16[7,28,2048]{2,1,0:T(8,128)(2,1)S(1)}, bf16[7,28,2048]{2,1,0:T(8,128)(2,1)}, u32[]{:S(2)}) copy-start(bf16[7,28,2048]{2,1,0:T(8,128)(2,1)} %get-tuple-element.86) | copy-start | bytes 2408452
  211.1 135.1 %all-reduce.10.cloned.1.call-start = ((), (), s32[]{:S(2)}) async-start(), calls=%async_computation.15 | async-start | bytes 3145728 | tf_op jit(solution)/shard_map/psum | solution.py:300
  252.7 3.1 copy-start.32
  256.8 2.3 copy-start.24
  256.8 2.3 copy-start.28
  256.9 37.6 %copy-start.5 = (f32[1,7,28,512]{3,2,1,0:T(8,128)S(1)}, f32[1,7,28,512]{3,2,1,0:T(8,128)}, u32[]{:S(2)}) copy-start(f32[1,7,28,512]{3,2,1,0:T(8,128)} %copy-done.4) | copy-start | bytes 1204228
  346.2 3.7 %copy-start.17 = (bf16[128,2048]{1,0:T(8,128)(2,1)S(1)}, bf16[128,2048]{1,0:T(8,128)(2,1)}, u32[]{:S(2)}) copy-start(bf16[128,2048]{1,0:T(8,128)(2,1)} %get-tuple-element.70) | copy-start | bytes 1572868
  346.2 4.7 %copy-start.16 = (bf16[512,512]{1,0:T(8,128)(2,1)S(1)}, bf16[512,512]{1,0:T(8,128)(2,1)}, u32[]{:S(2)}) copy-start(bf16[512,512]{1,0:T(8,128)(2,1)} %get-tuple-element.71) | copy-start | bytes 1572868
Sparse Core Ops, SparseCore 0:
  10.1 22.5 all-gather.8
  34.3 22.5 all-gather.10
  58.5 22.5 all-gather.12
  132.8 22.0 reduce-scatter.6
  157.2 31.1 reduce-scatter.8
  190.8 31.1 reduce-scatter.10
  224.6 28.0 reduce-scatter.4
  256.5 89.6 all-reduce.9
where the time goes:
time: 364 us; the launch traced here: 359 us
  waiting for transfers between devices  117 us (32%)
  blocking collectives  87.2 us (24%)
  local copies, waits for them, and re-layouts  70.8 us (19%)
  matrix products  37 us (10%)
  between operations  16.5 us (5%)
  starting transfers between devices  15.7 us (4%)
  other arithmetic  15.1 us (4%)
    psum x1, waiting for transfers between devices, shards(): lax.psum(shares[2].astype(jnp.bfloat16), 'seq').astype(jnp.float32)  50.3 us
    reduce_scatter x1, waiting for transfers between devices, shards(): lax.psum_scatter(qkv_grad_w.astype(jnp.bfloat16), 'fsdp', scatter_dimensi...  30.6 us
    unnamed x92, local copies, waits for them, and re-layouts  24.5 us
    psum x1, blocking collectives, shards(): lax.psum(shares[0].astype(jnp.bfloat16), 'seq').astype(jnp.float32)  21.9 us
    all_to_all x1, blocking collectives, shards(): lax.all_to_all(qkv_grad_heads, 'seq', split_axis=2, concat_axis=4, tiled=...  19.8 us
    all_gather x1, waiting for transfers between devices, shards(): lax.all_gather(qkv_weight, 'fsdp', axis=0, tiled=True)  10.7 us
    unnamed x1, blocking collectives  10.5 us
    reduce_scatter x1, waiting for transfers between devices, shards(): lax.psum_scatter(reduce_grad.astype(jnp.bfloat16), 'fsdp', scatter_dimens...  8.96 us
  transfers between devices with their start and end apart: 11, of which 6 were waited for; matrix products, arithmetic and copies ran while one was open for 28% of the time, Pallas kernels for 0%

commit v1 on v0

--- a/solution.py
+++ b/solution.py
@@ -1,3 +1,4 @@
+import functools
 import jax
 import jax.numpy as jnp
 from jax import lax
@@ -9,6 +10,19 @@
 MASKED = -100.0
 SQRT_HALF = 0.7071067811865476
 INV_ROOT_TAU = 0.3989422804014327
+
+
+def define_screen(content, device_axis):
+    top = jnp.concatenate(
+        jax.lax.all_to_all(
+            jnp.stack(jnp.split(content, jax.lax.axis_size(device_axis), axis=2)), device_axis, 0, 0
+        ),
+        axis=4,
+    )
+    return top
+
+
+carry_loads = functools.partial(define_screen, device_axis="seq")
 
 
 def layer_norm(values, norm_gain, norm_offset):
@@ -252,7 +266,7 @@
         grad_heads, kept_state, rel_bias, mask_add, per_device
     )
     qkv_grad_heads = jnp.roll(qkv_grad_heads, SHIFT, axis=2)
-    qkv_grad = lax.all_to_all(qkv_grad_heads, "seq", split_axis=2, concat_axis=4, tiled=True)
+    qkv_grad = carry_loads(qkv_grad_heads)
     table_part = table_grad(bias_grad, relative_index, entries)
     table_grads = lax.dynamic_update_slice(
         jnp.zeros((num_heads, entries), jnp.float32), table_part, (head_start, 0)

time: 364 us -> 364 us (level)
    unnamed x92 -> x98, local copies, waits for them, and re-layouts: 24.5 us -> 23.2 us
  transfers between devices with their start and end apart: 11 -> 11, of which waited for: 6 -> 6; matrix products, arithmetic and copies ran while one was open for 28% -> 29% of each run, Pallas kernels for 0% -> 0%
where the time goes in v1:
time: 364 us; the launch traced here: 359 us
  waiting for transfers between devices  117 us (32%)
  blocking collectives  86.9 us (24%)
  local copies, waits for them, and re-layouts  69.6 us (19%)
  matrix products  37 us (10%)
  between operations  16.5 us (5%)
  other arithmetic  16.2 us (4%)
  starting transfers between devices  15.7 us (4%)
    psum x1, waiting for transfers between devices, shards(): lax.psum(shares[2].astype(jnp.bfloat16), 'seq').astype(jnp.float32)  50.3 us
    reduce_scatter x1, waiting for transfers between devices, shards(): lax.psum_scatter(qkv_grad_w.astype(jnp.bfloat16), 'fsdp', scatter_dimensi...  30.6 us
    unnamed x98, local copies, waits for them, and re-layouts  23.2 us
    psum x1, blocking collectives, shards(): lax.psum(shares[0].astype(jnp.bfloat16), 'seq').astype(jnp.float32)  21.9 us
    all_to_all x1, blocking collectives, define_screen(): jax.lax.all_to_all(jnp.stack(jnp.split(content, jax.lax.axis_size(device_...  19.5 us
    reduce_scatter x1, waiting for transfers between devices, shards(): lax.psum_scatter(reduce_grad.astype(jnp.bfloat16), 'fsdp', scatter_dimens...  11.2 us
    all_gather x1, waiting for transfers between devices, shards(): lax.all_gather(qkv_weight, 'fsdp', axis=0, tiled=True)  10.7 us
    unnamed x1, blocking collectives  10.5 us
  transfers between devices with their start and end apart: 11, of which 6 were waited for; matrix products, arithmetic and copies ran while one was open for 29% of the time, Pallas kernels for 0%

profile of v1, /device:TPU:0, one launch (start us, length us, event | category | flops | bytes accessed | tf_op | source)
XLA Modules:
  0.0 359.1 jit_solution(6817626767328594070)
XLA Ops:
  7.2 2.0 copy.107
  10.0 6.2 %all-gather = bf16[4,1,128]{2,1,0:T(2,128)(2,1)S(1)} all-gather(bf16[1,1,128]{2,1,0:T(2,128)(2,1)} %bitcast.290), channel_id=1, replica_groups=mesh['fsdp'=4,'seq'=8] {'fsdp'}, dimensions={0}, use_global_device_ids=true | all-gather | bytes 1280 | tf_op jit(solution)/shard_map/all_gather | solution.py:185
  16.2 5.4 %all-gather.1 = bf16[4,1,128]{2,1,0:T(2,128)(2,1)S(1)} all-gather(bf16[1,1,128]{2,1,0:T(2,128)(2,1)} %bitcast.291), channel_id=1, replica_groups=mesh['fsdp'=4,'seq'=8] {'fsdp'}, dimensions={0}, use_global_device_ids=true | all-gather | bytes 1280 | tf_op jit(solution)/shard_map/all_gather | solution.py:186
  22.0 10.7 %all-gather.9.cloned.1.call-done = bf16[512,1536]{0,1:T(8,128)(2,1)} async-done(((bf16[128,1536]{0,1:T(8,128)(2,1)}), bf16[512,1536]{0,1:T(8,128)(2,1)}) %all-gather.9.cloned.1.call-update) | async-done | bytes 1572880 | tf_op jit(solution)/shard_map/all_gather | solution.py:187
  32.7 2.9 fusion.22
  35.6 3.7 %copy.109 = bf16[1,3,7,28,512]{3,2,1,0,4:T(8,128)(2,1)S(1)} copy(bf16[1,3,7,28,512]{4,3,1,2,0:T(8,128)(2,1)} %fusion.22) | data formatting | bytes 1204224 | tf_op jit(solution)/shard_map/convert_element_type | solution.py:217
  39.4 4.6 %reshape.411 = bf16[8,2,18816]{2,1,0:T(2,128)(2,1)} reshape(bf16[512,1,3,7,28]{4,3,2,1,0:T(8,128)(2,1)S(1)} %bitcast.256) | data formatting | bytes 1204224
  44.0 5.6 %all-to-all-start = ((bf16[8,2,18816]{2,1,0:T(2,128)(2,1)}), bf16[8,2,18816]{2,1,0:T(2,128)(2,1)}, u32[]{:S(2)}, u32[]{:S(2)}) async-start(bf16[8,2,18816]{2,1,0:T(2,128)(2,1)} %reshape.411), calls=%async_computation | async-start | bytes 1204224 | tf_op jit(solution)/shard_map/all_to_all | solution.py:218
  50.4 5.4 %all-gather.2 = bf16[4,4,169]{2,1,0:T(4,128)(2,1)S(1)} all-gather(bf16[1,4,169]{2,1,0:T(4,128)(2,1)S(1)} %bitcast.287), channel_id=1, replica_groups=mesh['fsdp'=4,'seq'=8] {'fsdp'}, dimensions={0}, use_global_device_ids=true | all-gather | bytes 6760 | tf_op jit(solution)/shard_map/all_gather | solution.py:189
  57.2 1.2 compare_select_fusion
  58.4 7.9 %all-to-all-done = bf16[8,2,18816]{2,1,0:T(2,128)(2,1)} async-done(((bf16[8,2,18816]{2,1,0:T(2,128)(2,1)}), bf16[8,2,18816]{2,1,0:T(2,128)(2,1)}, u32[]{:S(2)}, u32[]{:S(2)}) %all-to-all-start) | async-done | bytes 602144 | tf_op jit(solution)/shard_map/all_to_all | solution.py:218
  66.3 5.0 %reshape.412 = bf16[512,1,3,7,28]{4,3,2,1,0:T(8,128)(2,1)S(1)} reshape(bf16[8,2,18816]{2,1,0:T(2,128)(2,1)} %all-to-all-done) | data formatting | bytes 1204224
  71.3 4.5 %copy.110 = bf16[1,3,7,28,8,64]{5,2,4,3,1,0:T(8,128)(2,1)} copy(bf16[1,3,7,28,8,64]{3,2,1,5,4,0:T(8,128)(2,1)S(1)} %bitcast.255) | data formatting | bytes 1204224 | tf_op jit(solution)/shard_map/all_to_all | solution.py:218
  75.8 2.4 all_to_all.43
  79.0 1.3 fusion.27
  80.3 4.3 %reshape.361 = bf16[1,3,8,7,4,7,2,32]{7,6,3,2,5,4,1,0:T(2,128)(2,1)S(1)} reshape(bf16[1,3,56,28,64]{4,2,3,1,0:T(8,128)(2,1)} %fusion.27) | data formatting | bytes 1204224 | tf_op jit(solution)/shard_map/reshape | solution.py:56
  85.1 1.5 copy.160
  88.0 2.2 exponential_reduce_fusion
  90.2 1.2 convolution_convert_fusion.2
  91.4 1.6 copy.120
  93.0 1.5 copy.121
  94.5 2.2 reshape.368
  98.0 3.6 %all-to-all-start.1 = ((bf16[8,2,6272]{2,1,0:T(2,128)(2,1)}), bf16[8,2,6272]{2,1,0:T(2,128)(2,1)S(1)}, u32[]{:S(2)}, u32[]{:S(2)}) async-start(bf16[8,2,6272]{2,1,0:T(2,128)(2,1)} %reshape.413), calls=%async_computation.1 | async-start | bytes 401408 | tf_op jit(solution)/shard_map/all_to_all | solution.py:226
  101.7 5.1 %all-gather.3 = bf16[4,1,128]{2,1,0:T(2,128)(2,1)S(1)} all-gather(bf16[1,1,128]{2,1,0:T(2,128)(2,1)S(1)} %bitcast.292), channel_id=1, replica_groups=mesh['fsdp'=4,'seq'=8] {'fsdp'}, dimensions={0}, use_global_device_ids=true | all-gather | bytes 1280 | tf_op jit(solution)/shard_map/all_gather | solution.py:190
  106.8 5.0 %all-gather.4 = bf16[4,1,128]{2,1,0:T(2,128)(2,1)S(1)} all-gather(bf16[1,1,128]{2,1,0:T(2,128)(2,1)S(1)} %bitcast.293), channel_id=1, replica_groups=mesh['fsdp'=4,'seq'=8] {'fsdp'}, dimensions={0}, use_global_device_ids=true | all-gather | bytes 1280 | tf_op jit(solution)/shard_map/all_gather | solution.py:191
  112.4 7.9 %all_gather.31 = bf16[512,512]{1,0:T(8,128)(2,1)S(1)} all-gather(bf16[128,512]{1,0:T(8,128)(2,1)S(1)} %copy-done.20), channel_id=1, replica_groups=mesh['fsdp'=4,'seq'=8] {'fsdp'}, dimensions={0}, use_global_device_ids=true | all-gather | bytes 655360 | tf_op jit(solution)/shard_map/all_gather | solution.py:188
  121.8 4.0 %multiply_convert_fusion = (bf16[7,28,2048]{2,1,0:T(8,128)(2,1)}, f32[7,28,2048]{2,1,0:T(8,128)}) fusion(bf16[512,2048]{1,0:T(8,128)(2,1)} %all-gather.11.cloned.1.call-done, f32[1,7,28,512]{3,2,1,0:T(8,128)S(1)} %get-tuple-element.85, f32[512]{0:T(512)S(1)} %bitcast.286, f32[512]{0:T(512)S(1)} %bitcast.275, f32[7,28]{1,0:T(8,128)S(1)} %add_rsqrt_fusion, ...), kind=kOutput, calls=%fused_computation.32 | convolution fusion | flops 413550592 | bytes 4912672 | tf_op jit(solution)/shard_map/brwc,cf->brwf/dot_general | solution.py:232
  125.8 3.3 fusion.3
  129.2 1.4 fusion.64
  131.5 1.1 fusion.21
  132.7 3.4 bitcast_convert_fusion.1
  136.7 1.0 fusion.35
  137.8 1.8 copy.125
  139.5 1.9 reshape.415
  141.5 5.9 %all-to-all-start.2 = ((bf16[8,2,6272]{2,1,0:T(2,128)(2,1)}), bf16[8,2,6272]{2,1,0:T(2,128)(2,1)S(1)}, u32[]{:S(2)}, u32[]{:S(2)}) async-start(bf16[8,2,6272]{2,1,0:T(2,128)(2,1)} %reshape.415), calls=%async_computation.2 | async-start | bytes 401408 | tf_op jit(solution)/shard_map/all_to_all | solution.py:263
  147.4 3.4 bitcast_convert_fusion
  151.0 4.9 %all-to-all-done.2 = bf16[8,2,6272]{2,1,0:T(2,128)(2,1)S(1)} async-done(((bf16[8,2,6272]{2,1,0:T(2,128)(2,1)}), bf16[8,2,6272]{2,1,0:T(2,128)(2,1)S(1)}, u32[]{:S(2)}, u32[]{:S(2)}) %all-to-all-start.2) | async-done | bytes 200736 | tf_op jit(solution)/shard_map/all_to_all | solution.py:263
  155.9 1.1 reshape.416
  157.0 1.9 copy.126
  159.0 1.2 all_to_all.50
  161.9 2.0 copy.128
  163.8 1.4 convolution_convert_fusion
  165.2 2.5 copy.135
  169.9 1.4 copy.130
  171.4 1.4 convolution_convert_fusion.1
  172.8 1.7 copy.132
  175.0 1.9 copy.136
  176.9 2.5 reshape.375
  180.3 1.3 slice.120
  183.7 19.5 %all_to_all.56 = bf16[8,2,18816]{2,1,0:T(2,128)(2,1)S(1)} all-to-all(bf16[8,2,18816]{2,1,0:T(2,128)(2,1)S(1)} %reshape.417), channel_id=1, replica_groups=mesh['fsdp'=4,'seq'=8] {'seq'}, dimensions={0} | all-to-all | bytes 1204224 | tf_op jit(solution)/shard_map/all_to_all | solution.py:17
  206.9 1.9 fusion
  210.8 11.2 %reduce-scatter.11.cloned.1.call-done = bf16[512,512]{1,0:T(8,128)(2,1)} async-done(((bf16[2048,512]{1,0:T(8,128)(2,1)}), bf16[512,512]{1,0:T(8,128)(2,1)}) %reduce-scatter.11.cloned.1.call-update) | async-done | bytes 524304 | tf_op jit(solution)/shard_map/reduce_scatter | solution.py:307
  222.0 30.6 %reduce-scatter.5.cloned.1.call-done = bf16[128,1536]{1,0:T(8,128)(2,1)} async-done(((bf16[512,1536]{1,0:T(8,128)(2,1)}), bf16[128,1536]{1,0:T(8,128)(2,1)}) %reduce-scatter.5.cloned.1.call-update) | async-done | bytes 393232 | tf_op jit(solution)/shard_map/reduce_scatter | solution.py:289
  252.7 2.9 fusion.32
  255.7 1.1 fusion.37
  256.8 2.1 fusion.62
  259.1 10.5 %all-reduce.7 = (bf16[512]{0:T(512)(128)(2,1)S(1)}, bf16[512]{0:T(512)(128)(2,1)S(1)}, bf16[16,169]{1,0:T(8,128)(2,1)S(1)}, bf16[512]{0:T(512)(128)(2,1)S(1)}, bf16[512]{0:T(512)(128)(2,1)S(1)}) all-reduce(bf16[512]{0:T(512)(128)(2,1)S(1)} %get-tuple-element.57, ...), channel_id=2, replica_groups=mesh['fsdp'=4,'seq'=8] {'fsdp'}, use_global_device_ids=true, to_apply=%region_11.12.clone | all-reduce | flops 4752 | bytes 19008
  269.9 21.9 %all-reduce.5 = (bf16[128]{0:T(256)(128)(2,1)S(1)}, bf16[128]{0:T(256)(128)(2,1)S(1)}, bf16[4,169]{1,0:T(4,128)(2,1)S(1)}, bf16[128]{0:T(256)(128)(2,1)S(1)}, bf16[128]{0:T(256)(128)(2,1)S(1)}) all-reduce(bf16[128]{0:T(256)(128)(2,1)S(1)} %dynamic-slice.1, ...), channel_id=1, replica_groups=mesh['fsdp'=4,'seq'=8] {'seq'}, use_global_device_ids=true, to_apply=%region_12.13 | all-reduce | flops 1188 | bytes 4752 | tf_op jit(solution)/shard_map/psum | solution.py:312
  294.7 1.2 copy.143
  295.8 50.3 %all-reduce.10.cloned.1.call-done = (bf16[128,1536]{1,0:T(8,128)(2,1)}, bf16[128,512]{1,0:T(8,128)(2,1)}, bf16[128,2048]{1,0:T(8,128)(2,1)}, bf16[512,512]{1,0:T(8,128)(2,1)}) async-done(((bf16[128,1536]{1,0:T(8,128)(2,1)}, bf16[128,512]{1,0:T(8,128)(2,1)}, bf16[128,2048]{1,0:T(8,128)(2,1)}, bf16[512,512]{1,0:T(8,128)(2,1)}), (bf16[128,1536]{1,0:T(8,128)(2,1)}, bf16[128,512]{1,0:T(8,128)(2,1)}, ...) | async-done | bytes 1572880 | tf_op jit(solution)/shard_map/psum | solution.py:314
  346.1 1.7 convert_element_type.178
  347.9 2.0 convert_element_type.176
  349.8 1.1 convert_element_type.186
  350.9 1.1 convert_element_type.188
  (181 shorter events, 26.4 us)
Async XLA Ops:
  7.2 25.5 %copy-start.37 = (f32[3]{0:T(128)S(1)}, f32[3]{0:T(128)}, u32[]{:S(2)}) copy-start(f32[3]{0:T(128)} %constant.41.clone) | copy-start | bytes 40
  7.2 14.5 %copy-start.7 = (bf16[1,7,28,512]{3,2,1,0:T(8,128)(2,1)S(1)}, bf16[1,7,28,512]{3,2,1,0:T(8,128)(2,1)}, u32[]{:S(2)}) copy-start(bf16[1,7,28,512]{3,2,1,0:T(8,128)(2,1)} %param.14) | copy-start | bytes 602116
  7.2 25.5 %all-gather.9.cloned.1.call-start = ((), (), s32[]{:S(2)}) async-start(), calls=%async_computation.8 | async-start | bytes 1966080 | tf_op jit(solution)/shard_map/all_gather | solution.py:187
  9.2 112.5 %all-gather.11.cloned.1.call-start = ((), (), s32[]{:S(2)}) async-start(), calls=%async_computation.9 | async-start | bytes 2621440 | tf_op jit(solution)/shard_map/all_gather | solution.py:192
  16.2 16.5 %copy-start.21 = (f32[4,1,128]{2,1,0:T(1,128)}, f32[4,1,128]{2,1,0:T(1,128)S(1)}, u32[]{:S(2)}) copy-start(f32[4,1,128]{2,1,0:T(1,128)S(1)} %convert_element_type.189) | copy-start | bytes 6148
  21.7 11.1 %copy-start.29 = (f32[4,1,128]{2,1,0:T(1,128)}, f32[4,1,128]{2,1,0:T(1,128)S(1)}, u32[]{:S(2)}) copy-start(f32[4,1,128]{2,1,0:T(1,128)S(1)} %convert_element_type.190) | copy-start | bytes 6148
  22.0 10.7 %copy-start.23 = (f32[7,28]{1,0:T(8,128)}, f32[7,28]{1,0:T(8,128)S(1)}, u32[]{:S(2)}) copy-start(f32[7,28]{1,0:T(8,128)S(1)} %add_rsqrt_fusion.1) | copy-start | bytes 2356
  39.4 11.0 %copy-start.28 = (bf16[4,169]{1,0:T(4,128)(2,1)S(1)}, bf16[4,169]{1,0:T(4,128)(2,1)}, u32[]{:S(2)}) copy-start(bf16[4,169]{1,0:T(4,128)(2,1)} %param.22) | copy-start | bytes 4060
  39.4 16.4 %copy-start.34 = (s32[49,49]{1,0:T(8,128)S(1)}, s32[49,49]{1,0:T(8,128)}, u32[]{:S(2)}) copy-start(s32[49,49]{1,0:T(8,128)} %param.17) | copy-start | bytes 28816
  44.0 12.7 %copy-start.25 = (s32[56,28]{0,1:T(8,128)S(1)}, s32[56,28]{0,1:T(8,128)}, u32[]{:S(2)}) copy-start(s32[56,28]{0,1:T(8,128)} %param.16) | copy-start | bytes 18820
  44.0 22.3 %all-to-all-start = ((bf16[8,2,18816]{2,1,0:T(2,128)(2,1)}), bf16[8,2,18816]{2,1,0:T(2,128)(2,1)}, u32[]{:S(2)}, u32[]{:S(2)}) async-start(bf16[8,2,18816]{2,1,0:T(2,128)(2,1)} %reshape.411), calls=%async_computation | async-start | bytes 1204224 | tf_op jit(solution)/shard_map/all_to_all | solution.py:218
  49.6 76.2 %all-gather.13.cloned.1.call-start = ((), (), s32[]{:S(2)}) async-start(), calls=%async_computation.10 | async-start | bytes 2621440 | tf_op jit(solution)/shard_map/all_gather | solution.py:193
  87.3 2.9 copy-start.2
  88.0 2.2 copy-start
  88.0 2.2 copy-start.13
  96.7 5.0 %copy-start.32 = (bf16[128]{0:T(256)(128)(2,1)S(1)}, bf16[128]{0:T(256)(128)(2,1)}, u32[]{:S(2)}) copy-start(bf16[128]{0:T(256)(128)(2,1)} %param.23) | copy-start | bytes 772
  96.7 10.1 %copy-start.33 = (bf16[128]{0:T(256)(128)(2,1)S(1)}, bf16[128]{0:T(256)(128)(2,1)}, u32[]{:S(2)}) copy-start(bf16[128]{0:T(256)(128)(2,1)} %param.24) | copy-start | bytes 772
  96.7 15.7 %copy-start.20 = (bf16[128,512]{1,0:T(8,128)(2,1)S(1)}, bf16[128,512]{1,0:T(8,128)(2,1)}, u32[]{:S(2)}) copy-start(bf16[128,512]{1,0:T(8,128)(2,1)} %param.21) | copy-start | bytes 393220
  98.0 22.3 %all-to-all-start.1 = ((bf16[8,2,6272]{2,1,0:T(2,128)(2,1)}), bf16[8,2,6272]{2,1,0:T(2,128)(2,1)S(1)}, u32[]{:S(2)}, u32[]{:S(2)}) async-start(bf16[8,2,6272]{2,1,0:T(2,128)(2,1)} %reshape.413), calls=%async_computation.1 | async-start | bytes 401408 | tf_op jit(solution)/shard_map/all_to_all | solution.py:226
  101.6 109.1 %reduce-scatter.7.cloned.1.call-start = ((), (), s32[]{:S(2)}) async-start(), calls=%async_computation.12 | async-start | bytes 655360 | tf_op jit(solution)/shard_map/reduce_scatter | solution.py:292
  112.4 8.8 %copy-start.8 = (bf16[1,7,28,512]{3,2,1,0:T(8,128)(2,1)S(1)}, bf16[1,7,28,512]{3,2,1,0:T(8,128)(2,1)}, u32[]{:S(2)}) copy-start(bf16[1,7,28,512]{3,2,1,0:T(8,128)(2,1)} %param.14) | copy-start | bytes 602116
  120.8 1.0 copy-start.26
  121.8 4.0 %copy-start.18 = (bf16[1,7,28,512]{3,2,1,0:T(8,128)(2,1)S(1)}, bf16[1,7,28,512]{3,2,1,0:T(8,128)(2,1)}, u32[]{:S(2)}) copy-start(bf16[1,7,28,512]{3,2,1,0:T(8,128)(2,1)} %param.15) | copy-start | bytes 602116
  125.8 3.3 copy-start.12
  129.1 1.4 copy-start.38
  129.1 2.1 copy-start.19
  131.5 5.3 %copy-start.4 = (f32[1,7,28,512]{3,2,1,0:T(8,128)}, f32[1,7,28,512]{3,2,1,0:T(8,128)S(1)}, u32[]{:S(2)}) copy-start(f32[1,7,28,512]{3,2,1,0:T(8,128)S(1)} %fusion.67) | copy-start | bytes 1204228
  132.6 78.2 %reduce-scatter.9.cloned.1.call-start = ((), (), s32[]{:S(2)}) async-start(), calls=%async_computation.13 | async-start | bytes 2621440 | tf_op jit(solution)/shard_map/reduce_scatter | solution.py:304
  141.5 14.4 %all-to-all-start.2 = ((bf16[8,2,6272]{2,1,0:T(2,128)(2,1)}), bf16[8,2,6272]{2,1,0:T(2,128)(2,1)S(1)}, u32[]{:S(2)}, u32[]{:S(2)}) async-start(bf16[8,2,6272]{2,1,0:T(2,128)(2,1)} %reshape.415), calls=%async_computation.2 | async-start | bytes 401408 | tf_op jit(solution)/shard_map/all_to_all | solution.py:263
  147.4 74.6 %reduce-scatter.11.cloned.1.call-start = ((), (), s32[]{:S(2)}) async-start(), calls=%async_computation.14 | async-start | bytes 2621440 | tf_op jit(solution)/shard_map/reduce_scatter | solution.py:307
  150.8 101.8 %reduce-scatter.5.cloned.1.call-start = ((), (), s32[]{:S(2)}) async-start(), calls=%async_computation.11 | async-start | bytes 1966080 | tf_op jit(solution)/shard_map/reduce_scatter | solution.py:289
  160.5 3.3 copy-start.15
  163.8 3.9 %copy-start.14 = (bf16[1,1,8,4,2,49,32]{5,6,4,3,2,1,0:T(8,128)(2,1)S(1)}, bf16[1,1,8,4,2,49,32]{5,6,4,3,2,1,0:T(8,128)(2,1)}, u32[]{:S(2)}) copy-start(bf16[1,1,8,4,2,49,32]{5,6,4,3,2,1,0:T(8,128)(2,1)} %copy.160) | copy-start | bytes 602116
  168.5 1.0 copy-start.3
  169.1 2.2 copy-start.1
  171.4 3.1 copy-start.10
  172.8 1.7 copy-start.11
  205.5 1.4 copy-start.9
  205.5 1.4 copy-start.22
  205.5 1.4 copy-start.24
  205.5 1.4 copy-start.30
  206.9 2.0 copy-start.36
  208.8 43.9 %copy-start.6 = (bf16[7,28,2048]{2,1,0:T(8,128)(2,1)S(1)}, bf16[7,28,2048]{2,1,0:T(8,128)(2,1)}, u32[]{:S(2)}) copy-start(bf16[7,28,2048]{2,1,0:T(8,128)(2,1)} %get-tuple-element.86) | copy-start | bytes 2408452
  208.8 137.3 %all-reduce.10.cloned.1.call-start = ((), (), s32[]{:S(2)}) async-start(), calls=%async_computation.15 | async-start | bytes 3145728 | tf_op jit(solution)/shard_map/psum | solution.py:314
  252.7 3.1 copy-start.35
  256.8 2.3 copy-start.27
  256.8 2.3 copy-start.31
  256.8 37.6 %copy-start.5 = (f32[1,7,28,512]{3,2,1,0:T(8,128)S(1)}, f32[1,7,28,512]{3,2,1,0:T(8,128)}, u32[]{:S(2)}) copy-start(f32[1,7,28,512]{3,2,1,0:T(8,128)} %copy-done.4) | copy-start | bytes 1204228
  346.1 3.7 %copy-start.17 = (bf16[128,2048]{1,0:T(8,128)(2,1)S(1)}, bf16[128,2048]{1,0:T(8,128)(2,1)}, u32[]{:S(2)}) copy-start(bf16[128,2048]{1,0:T(8,128)(2,1)} %get-tuple-element.70) | copy-start | bytes 1572868
  346.1 4.7 %copy-start.16 = (bf16[512,512]{1,0:T(8,128)(2,1)S(1)}, bf16[512,512]{1,0:T(8,128)(2,1)}, u32[]{:S(2)}) copy-start(bf16[512,512]{1,0:T(8,128)(2,1)} %get-tuple-element.71) | copy-start | bytes 1572868
Sparse Core Ops, SparseCore 0:
  10.1 22.5 all-gather.8
  34.3 22.5 all-gather.10
  58.5 22.5 all-gather.12
  132.7 22.0 reduce-scatter.6
  157.3 31.1 reduce-scatter.8
  190.8 31.1 reduce-scatter.10
  224.5 28.0 reduce-scatter.4
  256.4 89.6 all-reduce.9
